TPU v7x, 512 devices: a whole 4x8x8 slice. The times are simulated.
512 devices in a mesh: ctx: 128 (over y, x_hi, z), head: 4 (over x_lo, core).
Axes of the slice: x: 4 (x_hi: 2, x_lo: 2; x = x_hi * 2 + x_lo), y: 8, z: 8, core: 2. Of those that a mesh axis runs over, the one named last changes fastest.
Arguments:
- text_query: bfloat16 [16384, 2560], P('ctx', 'head')
- grad_out: bfloat16 [16384, 2560], P('ctx', 'head'), may hold values from -6 to 6
- frame_kv: bfloat16 [2, 65536, 2560], P(None, 'ctx', 'head')
- sink_logit: float32 [20], P('head'), may hold values from 1 to 6
- pairing: int32 [128], replicated, may hold values from 0 to 127, each once
- block_mask: int32 [128, 4], P('ctx'), may hold values from 0 to 1
- text_seg: int32 [16384], P('ctx'), may hold values from 0 to 3, as said below
- frame_seg: int32 [65536], P('ctx'), may hold values from 0 to 3, as said below
Outputs:
- grad_query: bfloat16 [16384, 2560], P('ctx', 'head')
- grad_kv: bfloat16 [2, 65536, 2560], P(None, ('ctx', 'head'))
Inputs may be any that keep to these rules, and one draw needn't show every extreme that they name: pairing is a permutation of the ctx indices. `text_seg`: within the 128 text tokens of each ctx index the ids do not fall and each of the 4 ids appears. `frame_seg`: within the 512 frames of each ctx index the ids do not fall and each of the 4 ids appears.
All inputs are finite; a program needn't handle non-finite values.
Results may differ from a plain program's by a relative error of at most 0.0081.
Values may be sent and summed in bfloat16 or wider, within the bound.
A program may use at most 64 MiB of HBM per device.

v0:
```python
import jax
import jax.numpy as jnp
from jax import lax
from jax.sharding import PartitionSpec as P

DH = 128
BLOCK = 128


def attend(query_rows, grad_rows, key_rows, value_rows, row_mask, text_ids, frame_ids, sink_logit):
    score_scale = DH ** (-0.5)
    text_rows = query_rows.shape[0]
    frame_rows = key_rows.shape[0]
    head_count = query_rows.shape[1] // DH
    q_heads = query_rows.reshape(text_rows, head_count, DH)
    g_heads = grad_rows.reshape(text_rows, head_count, DH)
    k_heads = key_rows.reshape(frame_rows, head_count, DH)
    v_heads = value_rows.reshape(frame_rows, head_count, DH)
    allowed = (jnp.repeat(row_mask, BLOCK, axis=1) == 1) & (text_ids[:, None] == frame_ids[None, :])
    scores = (
        jnp.einsum("the,fhe->htf", q_heads, k_heads, preferred_element_type=jnp.float32)
        * score_scale
    )
    masked = jnp.where(allowed[None], scores, -1e30)
    row_top = jnp.maximum(sink_logit[:, None], jnp.max(masked, axis=2))
    exp_terms = jnp.where(allowed[None], jnp.exp(masked - row_top[:, :, None]), 0.0)
    row_total = jnp.exp(sink_logit[:, None] - row_top) + jnp.sum(exp_terms, axis=2)
    attention = exp_terms / row_total[:, :, None]
    attention_low = attention.astype(jnp.bfloat16)
    output = jnp.einsum("htf,fhe->the", attention_low, v_heads, preferred_element_type=jnp.float32)
    grad_attention = jnp.einsum(
        "the,fhe->htf", g_heads, v_heads, preferred_element_type=jnp.float32
    )
    row_delta = jnp.sum(g_heads.astype(jnp.float32) * output, axis=2)
    grad_scores = (attention * (grad_attention - row_delta.T[:, :, None])).astype(jnp.bfloat16)
    grad_query = (
        jnp.einsum("htf,fhe->the", grad_scores, k_heads, preferred_element_type=jnp.float32)
        * score_scale
    )
    grad_keys = (
        jnp.einsum("htf,the->fhe", grad_scores, q_heads, preferred_element_type=jnp.float32)
        * score_scale
    )
    grad_values = jnp.einsum(
        "htf,the->fhe", attention_low, g_heads, preferred_element_type=jnp.float32
    )
    grad_pair = jnp.stack([grad_keys.reshape(frame_rows, -1), grad_values.reshape(frame_rows, -1)])
    return (grad_query.reshape(text_rows, -1).astype(jnp.bfloat16), grad_pair.astype(jnp.bfloat16))


def shards(text_query, grad_out, frame_kv, sink_logit, pairing, block_mask, text_seg, frame_seg):
    owners = lax.axis_size("ctx")
    text_rows = text_query.shape[0]
    feature_width = text_query.shape[1]
    frame_blocks = block_mask.shape[1]
    indices = jnp.arange(owners, dtype=jnp.int32)
    inverse = jnp.sum(jnp.where(pairing[None, :] == indices[:, None], indices[None, :], 0), axis=1)
    row_mask = jnp.repeat(block_mask, BLOCK, axis=0)
    stacked = jnp.stack([text_query, grad_out]).reshape(
        2, owners, text_rows // owners, feature_width
    )
    text_tags = jnp.concatenate([text_seg[:, None], row_mask], axis=1).astype(jnp.bfloat16)
    text_tags = text_tags.reshape(1, owners, text_rows // owners, frame_blocks + 1)
    first_text, first_tags = (
        lax.all_to_all(stacked, "ctx", split_axis=1, concat_axis=1, tiled=True),
        lax.all_to_all(text_tags, "ctx", split_axis=1, concat_axis=1, tiled=True),
    )
    second_text, second_tags = (
        lax.all_to_all(
            jnp.take(first_text, inverse, axis=1), "ctx", split_axis=1, concat_axis=1, tiled=True
        ),
        lax.all_to_all(
            jnp.take(first_tags, inverse, axis=1), "ctx", split_axis=1, concat_axis=1, tiled=True
        ),
    )
    visiting = second_text.reshape(2, text_rows, feature_width)
    visiting_tags = second_tags.reshape(text_rows, frame_blocks + 1).astype(jnp.int32)
    grad_visit, home_adjoint = attend(
        visiting[0],
        visiting[1],
        frame_kv[0],
        frame_kv[1],
        visiting_tags[:, 1:],
        visiting_tags[:, 0],
        frame_seg,
        sink_logit,
    )
    returning = lax.all_to_all(
        grad_visit.reshape(1, owners, text_rows // owners, feature_width),
        "ctx",
        split_axis=1,
        concat_axis=1,
        tiled=True,
    )
    grad_query = lax.all_to_all(
        jnp.take(returning, pairing, axis=1), "ctx", split_axis=1, concat_axis=1, tiled=True
    ).reshape(text_rows, feature_width)
    grad_kv = lax.all_to_all(home_adjoint, "head", split_axis=1, concat_axis=2, tiled=True)
    return (grad_query, grad_kv)


def solution(mesh):
    in_specs = (
        P("ctx", "head"),
        P("ctx", "head"),
        P(None, "ctx", "head"),
        P("head"),
        P(),
        P("ctx", None),
        P("ctx"),
        P("ctx"),
    )
    out_specs = (P("ctx", "head"), P(None, ("ctx", "head"), None))
    return jax.shard_map(shards, mesh=mesh, in_specs=in_specs, out_specs=out_specs, check_vma=False)
```

profile of v0, /device:TPU:1, one launch (start us, length us, event | category | flops | bytes accessed | tf_op | source)
XLA Modules:
  0.0 181.7 jit_solution(7947610529917276390)
XLA Ops:
  0.7 0.8 convert_bitcast_fusion
  1.4 0.7 convert_bitcast_fusion.1
  2.1 0.1 pad.5.clone
  2.1 0.1 pad_maximum_fusion.1
  2.2 0.8 copy.78
  3.0 20.8 %all-to-all-start = ((bf16[1,128,1,5]{3,2,0,1:T(2,128)(2,1)}), bf16[1,128,1,5]{3,2,0,1:T(2,128)(2,1)S(1)}, u32[]{:S(2)}, u32[]{:S(2)}) async-start(bf16[1,128,1,5]{3,2,0,1:T(2,128)(2,1)} %copy.78), calls=%async_computation | async-start | bytes 131072 | tf_op jit(solution)/shard_map/all_to_all | solution.py:66
  23.8 0.8 select_reduce_fusion
  24.6 1.0 maximum_bitcast_fusion
  25.6 1.1 copy.82
  26.7 10.0 %all-to-all-done = bf16[1,128,1,5]{3,2,0,1:T(2,128)(2,1)S(1)} async-done(((bf16[1,128,1,5]{3,2,0,1:T(2,128)(2,1)}), bf16[1,128,1,5]{3,2,0,1:T(2,128)(2,1)S(1)}, u32[]{:S(2)}, u32[]{:S(2)}) %all-to-all-start) | async-done | bytes 1312 | tf_op jit(solution)/shard_map/all_to_all | solution.py:66
  36.8 6.2 %all-to-all-start.2 = ((bf16[2,128,1,640]{3,0,2,1:T(2,128)(2,1)}), bf16[2,128,1,640]{3,0,2,1:T(2,128)(2,1)S(1)}, u32[]{:S(2)}, u32[]{:S(2)}) async-start(bf16[2,128,1,640]{3,0,2,1:T(2,128)(2,1)} %copy.82), calls=%async_computation.2 | async-start | bytes 655360 | tf_op jit(solution)/shard_map/all_to_all | solution.py:65
  43.0 0.1 fusion.15
  43.1 0.7 gather_fusion
  43.8 0.1 bitcast_select_fusion.1
  43.9 0.7 copy.81
  44.6 13.1 %all-to-all-done.2 = bf16[2,128,1,640]{3,0,2,1:T(2,128)(2,1)S(1)} async-done(((bf16[2,128,1,640]{3,0,2,1:T(2,128)(2,1)}), bf16[2,128,1,640]{3,0,2,1:T(2,128)(2,1)S(1)}, u32[]{:S(2)}, u32[]{:S(2)}) %all-to-all-start.2) | async-done | bytes 327712 | tf_op jit(solution)/shard_map/all_to_all | solution.py:65
  57.7 8.6 %all-to-all-start.1 = ((bf16[1,128,1,5]{3,2,0,1:T(2,128)(2,1)}), bf16[1,128,1,5]{3,2,0,1:T(2,128)(2,1)S(1)}, u32[]{:S(2)}, u32[]{:S(2)}) async-start(bf16[1,128,1,5]{3,2,0,1:T(2,128)(2,1)} %copy.81), calls=%async_computation.1 | async-start | bytes 131072 | tf_op jit(solution)/shard_map/all_to_all | solution.py:72
  66.3 1.3 gather_fusion.1
  67.5 1.1 fusion.11
  68.7 10.5 %all-to-all-done.1 = bf16[1,128,1,5]{3,2,0,1:T(2,128)(2,1)S(1)} async-done(((bf16[1,128,1,5]{3,2,0,1:T(2,128)(2,1)}), bf16[1,128,1,5]{3,2,0,1:T(2,128)(2,1)S(1)}, u32[]{:S(2)}, u32[]{:S(2)}) %all-to-all-start.1) | async-done | bytes 1312 | tf_op jit(solution)/shard_map/all_to_all | solution.py:72
  79.2 6.4 %all-to-all-start.3 = ((bf16[2,128,1,640]{3,0,2,1:T(2,128)(2,1)}), bf16[2,128,1,640]{3,0,2,1:T(2,128)(2,1)S(1)}, u32[]{:S(2)}, u32[]{:S(2)}) async-start(bf16[2,128,1,640]{3,0,2,1:T(2,128)(2,1)} %fusion.11), calls=%async_computation.3 | async-start | bytes 655360 | tf_op jit(solution)/shard_map/all_to_all | solution.py:69
  85.6 0.3 copy.105
  85.8 0.3 copy.107
  86.1 0.1 convert_element_type.48
  86.2 0.1 slice_reduce_fusion
  86.3 0.1 slice_compare_fusion
  86.4 0.2 broadcast_in_dim.83
  86.6 0.1 bitcast_and_fusion
  86.7 13.5 %all-to-all-done.3 = bf16[2,128,1,640]{3,0,2,1:T(2,128)(2,1)S(1)} async-done(((bf16[2,128,1,640]{3,0,2,1:T(2,128)(2,1)}), bf16[2,128,1,640]{3,0,2,1:T(2,128)(2,1)S(1)}, u32[]{:S(2)}, u32[]{:S(2)}) %all-to-all-start.3) | async-done | bytes 327712 | tf_op jit(solution)/shard_map/all_to_all | solution.py:69
  100.2 0.5 fusion.16
  100.6 0.2 copy.104
  100.9 0.2 copy.106
  101.1 0.5 fusion.17
  101.6 0.1 broadcast_maximum_fusion
  101.7 0.4 fusion.8
  102.1 0.1 exponential_add_fusion
  102.2 0.6 fusion.6
  102.8 1.5 fusion.2
  104.3 0.3 fusion.5
  104.7 0.2 copy.92
  104.9 0.6 broadcast.200
  105.5 1.6 reduce.2
  107.1 0.9 reshape.298
  107.9 8.0 %all-to-all-start.4 = ((bf16[128,2,320]{2,1,0:T(2,128)(2,1)}), bf16[128,2,320]{2,1,0:T(2,128)(2,1)S(1)}, u32[]{:S(2)}, u32[]{:S(2)}) async-start(bf16[128,2,320]{2,1,0:T(2,128)(2,1)} %reshape.298), calls=%async_computation.4 | async-start | bytes 393216 | tf_op jit(solution)/shard_map/all_to_all | solution.py:88
  115.9 1.4 convolution_convert_fusion
  117.4 12.5 %all-to-all-done.4 = bf16[128,2,320]{2,1,0:T(2,128)(2,1)S(1)} async-done(((bf16[128,2,320]{2,1,0:T(2,128)(2,1)}), bf16[128,2,320]{2,1,0:T(2,128)(2,1)S(1)}, u32[]{:S(2)}, u32[]{:S(2)}) %all-to-all-start.4) | async-done | bytes 163872 | tf_op jit(solution)/shard_map/all_to_all | solution.py:88
  129.9 0.3 reshape.299
  130.2 0.9 gather_fusion.2
  131.1 0.1 bitcast_select_fusion
  131.2 0.3 copy.117
  131.4 1.6 reduce.3
  133.1 0.9 reshape.300
  133.9 7.4 %all-to-all-start.5 = ((bf16[128,2,320]{2,1,0:T(2,128)(2,1)}), bf16[128,2,320]{2,1,0:T(2,128)(2,1)}, u32[]{:S(2)}, u32[]{:S(2)}) async-start(bf16[128,2,320]{2,1,0:T(2,128)(2,1)} %reshape.300), calls=%async_computation.5 | async-start | bytes 393216 | tf_op jit(solution)/shard_map/all_to_all | solution.py:95
  141.3 0.3 fusion.3
  141.7 1.1 copy.95
  142.8 1.1 copy.94
  144.0 4.0 %pad_maximum_fusion = bf16[2,512,640]{2,0,1:T(2,128)(2,1)} fusion(bf16[1,512,640]{2,0,1:T(2,128)(2,1)S(1)} %copy.95, bf16[1,512,640]{2,0,1:T(2,128)(2,1)S(1)} %copy.94), kind=kLoop, calls=%fused_computation.11 | loop fusion | flops 2621440 | bytes 2621440 | tf_op jit(solution)/shard_map/stack | solution.py:47
  148.0 6.6 %all-to-all-done.5 = bf16[128,2,320]{2,1,0:T(2,128)(2,1)} async-done(((bf16[128,2,320]{2,1,0:T(2,128)(2,1)}), bf16[128,2,320]{2,1,0:T(2,128)(2,1)}, u32[]{:S(2)}, u32[]{:S(2)}) %all-to-all-start.5) | async-done | bytes 163872 | tf_op jit(solution)/shard_map/all_to_all | solution.py:95
  154.6 8.3 %all-to-all-start.6 = ((bf16[2,512,640]{2,0,1:T(2,128)(2,1)}), bf16[2,512,640]{2,0,1:T(2,128)(2,1)S(1)}, u32[]{:S(2)}, u32[]{:S(2)}) async-start(bf16[2,512,640]{2,0,1:T(2,128)(2,1)} %pad_maximum_fusion), calls=%async_computation.6 | async-start | bytes 2621440 | tf_op jit(solution)/shard_map/all_to_all | solution.py:98
  162.9 1.6 reshape.301
  164.6 0.7 copy.114
  165.3 14.1 %all-to-all-done.6 = bf16[2,512,640]{2,0,1:T(2,128)(2,1)S(1)} async-done(((bf16[2,512,640]{2,0,1:T(2,128)(2,1)}), bf16[2,512,640]{2,0,1:T(2,128)(2,1)S(1)}, u32[]{:S(2)}, u32[]{:S(2)}) %all-to-all-start.6) | async-done | bytes 1310752 | tf_op jit(solution)/shard_map/all_to_all | solution.py:98
  179.3 1.0 copy.96
  180.4 1.4 all_to_all.40
  (22 shorter events, 0.1 us)
Async XLA Ops:
  0.6 42.3 %copy-start.6 = (s32[128]{0:T(128)S(1)}, s32[128]{0:T(128)}, u32[]{:S(2)}) copy-start(s32[128]{0:T(128)} %param.12) | copy-start | bytes 1540
  0.6 42.3 %copy-start = (bf16[2,512,640]{2,1,0:T(8,128)(2,1)S(1)}, bf16[2,512,640]{2,1,0:T(8,128)(2,1)}, u32[]{:S(2)}) copy-start(bf16[2,512,640]{2,1,0:T(8,128)(2,1)} %param.10) | copy-start | bytes 3932164
  3.0 33.8 %all-to-all-start = ((bf16[1,128,1,5]{3,2,0,1:T(2,128)(2,1)}), bf16[1,128,1,5]{3,2,0,1:T(2,128)(2,1)S(1)}, u32[]{:S(2)}, u32[]{:S(2)}) async-start(bf16[1,128,1,5]{3,2,0,1:T(2,128)(2,1)} %copy.78), calls=%async_computation | async-start | bytes 131072 | tf_op jit(solution)/shard_map/all_to_all | solution.py:66
  36.8 20.9 %all-to-all-start.2 = ((bf16[2,128,1,640]{3,0,2,1:T(2,128)(2,1)}), bf16[2,128,1,640]{3,0,2,1:T(2,128)(2,1)S(1)}, u32[]{:S(2)}, u32[]{:S(2)}) async-start(bf16[2,128,1,640]{3,0,2,1:T(2,128)(2,1)} %copy.82), calls=%async_computation.2 | async-start | bytes 655360 | tf_op jit(solution)/shard_map/all_to_all | solution.py:65
  57.7 21.5 %all-to-all-start.1 = ((bf16[1,128,1,5]{3,2,0,1:T(2,128)(2,1)}), bf16[1,128,1,5]{3,2,0,1:T(2,128)(2,1)S(1)}, u32[]{:S(2)}, u32[]{:S(2)}) async-start(bf16[1,128,1,5]{3,2,0,1:T(2,128)(2,1)} %copy.81), calls=%async_computation.1 | async-start | bytes 131072 | tf_op jit(solution)/shard_map/all_to_all | solution.py:72
  79.2 21.0 %all-to-all-start.3 = ((bf16[2,128,1,640]{3,0,2,1:T(2,128)(2,1)}), bf16[2,128,1,640]{3,0,2,1:T(2,128)(2,1)S(1)}, u32[]{:S(2)}, u32[]{:S(2)}) async-start(bf16[2,128,1,640]{3,0,2,1:T(2,128)(2,1)} %fusion.11), calls=%async_computation.3 | async-start | bytes 655360 | tf_op jit(solution)/shard_map/all_to_all | solution.py:69
  85.6 1.0 copy-start.4
  100.9 0.7 copy-start.5
  101.1 1.1 copy-start.2
  104.3 11.6 %copy-start.3 = (bf16[1,128,1,640]{1,3,2,0:T(8,128)(2,1)S(1)}, bf16[1,128,1,640]{1,3,2,0:T(8,128)(2,1)}, u32[]{:S(2)}) copy-start(bf16[1,128,1,640]{1,3,2,0:T(8,128)(2,1)} %copy-done.2) | copy-start | bytes 491524
  107.9 21.9 %all-to-all-start.4 = ((bf16[128,2,320]{2,1,0:T(2,128)(2,1)}), bf16[128,2,320]{2,1,0:T(2,128)(2,1)S(1)}, u32[]{:S(2)}, u32[]{:S(2)}) async-start(bf16[128,2,320]{2,1,0:T(2,128)(2,1)} %reshape.298), calls=%async_computation.4 | async-start | bytes 393216 | tf_op jit(solution)/shard_map/all_to_all | solution.py:88
  131.4 10.2 %copy-start.1 = (bf16[5,128,512]{2,1,0:T(8,128)(2,1)S(1)}, bf16[5,128,512]{2,1,0:T(8,128)(2,1)}, u32[]{:S(2)}) copy-start(bf16[5,128,512]{2,1,0:T(8,128)(2,1)} %convolution_convert_fusion) | copy-start | bytes 1966084
  133.9 20.7 %all-to-all-start.5 = ((bf16[128,2,320]{2,1,0:T(2,128)(2,1)}), bf16[128,2,320]{2,1,0:T(2,128)(2,1)}, u32[]{:S(2)}, u32[]{:S(2)}) async-start(bf16[128,2,320]{2,1,0:T(2,128)(2,1)} %reshape.300), calls=%async_computation.5 | async-start | bytes 393216 | tf_op jit(solution)/shard_map/all_to_all | solution.py:95
  154.6 24.7 %all-to-all-start.6 = ((bf16[2,512,640]{2,0,1:T(2,128)(2,1)}), bf16[2,512,640]{2,0,1:T(2,128)(2,1)S(1)}, u32[]{:S(2)}, u32[]{:S(2)}) async-start(bf16[2,512,640]{2,0,1:T(2,128)(2,1)} %pad_maximum_fusion), calls=%async_computation.6 | async-start | bytes 2621440 | tf_op jit(solution)/shard_map/all_to_all | solution.py:98
where the time goes:
time: 182 us
  waiting for transfers between devices  80.3 us (44%)
  starting transfers between devices  65.6 us (36%)
  local copies, waits for them, and re-layouts  17.5 us (10%)
  other arithmetic  12.7 us (7%)
  matrix products  4.67 us (3%)
    all_to_all x1, starting transfers between devices, shards(): lax.all_to_all(text_tags, 'ctx', split_axis=1, concat_axis=1, tiled=True)  20.8 us
    all_to_all x1, waiting for transfers between devices, shards(): lax.all_to_all(home_adjoint, 'head', split_axis=1, concat_axis=2, tiled=T...  14.1 us
    all_to_all x1, waiting for transfers between devices, shards(): lax.all_to_all(jnp.take(first_text, inverse, axis=1), 'ctx', split_axis=1...  13.5 us
    all_to_all x1, waiting for transfers between devices, shards(): lax.all_to_all(stacked, 'ctx', split_axis=1, concat_axis=1, tiled=True)  13.1 us
    all_to_all x1, waiting for transfers between devices, shards(): lax.all_to_all(grad_visit.reshape(1, owners, text_rows // owners, feature...  12.5 us
    all_to_all x1, waiting for transfers between devices, shards(): lax.all_to_all(jnp.take(first_tags, inverse, axis=1), 'ctx', split_axis=1...  10.5 us
    all_to_all x1, waiting for transfers between devices, shards(): lax.all_to_all(text_tags, 'ctx', split_axis=1, concat_axis=1, tiled=True)  10 us
    all_to_all x1, starting transfers between devices, shards(): lax.all_to_all(jnp.take(first_tags, inverse, axis=1), 'ctx', split_axis=1...  8.58 us
  transfers between devices with their start and end apart: 7, of which 7 were waited for; matrix products, arithmetic and copies ran while one was open for 10% of the time, Pallas kernels for 0%

commit v1 on v0

v1 whole, which is shorter than its diff:
```python
import functools

import jax
import jax.numpy as jnp
from jax import lax
from jax.experimental import pallas as pl
from jax.experimental.pallas import tpu as pltpu
from jax.sharding import PartitionSpec as P

DH = 128
BLOCK = 128
TILE = 16
GROUPS = ((0, 1), (1, 1), (2, 1), (3, 1), (4, 1))
MESH = pl.DeviceIdType.MESH


def _dot(a, b, ca, cb):
    return lax.dot_general(a, b, (((ca,), (cb,)), ((), ())), preferred_element_type=jnp.float32)


def kernel(
    A, B, H,
    q_hbm, g_hbm, kv_hbm, sink, pair_s, pair_v, mask_v, tseg_v, fseg_v,
    dq_out, dkv_out,
    qg, kv, s1, s2, p3, s3, qr, dkv, dq, r1, r2, rp, r3, tag, ta, tb, fcol, inv_v, inv_s,
    in_sem, inv_sem,
    s1s, s1r, s2s, s2r, s3s, s3r, s4s, s4r,
    ks, kr, r1s, r1r, r2s, r2r, r3s, r3r, r4s, r4r,
    tas, tar, tbs, tbr,
):
    scale = DH ** (-0.5)
    c = lax.axis_index("ctx")
    j = lax.axis_index("head")
    a = c // B
    b = c % B
    core = j % 2
    heads_here = q_hbm.shape[1] // DH
    frames = kv_hbm.shape[1]
    frame_part = frames // H
    n_ctx = A * B

    def on_a(x):
        return {"ctx": x * B + b}

    def on_b(x):
        return {"ctx": a * B + x}

    def member(v):
        v = v % B
        return (v % 2) * (B // 2) + v // 2

    def text_member(i, kind):
        return member(2 * i + kind + 10 * core + 2 * a)

    def grad_member(i):
        return member(3 * i + 8 * core + 2 * a)

    def cols(i):
        first, count = GROUPS[i]
        return slice(first * DH, (first + count) * DH)

    def rows(x):
        return pl.ds(pl.multiple_of(x * TILE, TILE), TILE)

    def send(src, dst, ssem, rsem, where):
        pltpu.make_async_remote_copy(
            src_ref=src, dst_ref=dst, send_sem=ssem, recv_sem=rsem, device_id=where, device_id_type=MESH
        ).start()

    def local(src, dst, sem):
        pltpu.make_async_copy(src, dst, sem).start()

    def wait(ref, sem):
        pltpu.make_async_copy(ref, ref, sem).wait()

    def others(count, me, body):
        def step(k, carry):
            body((me + k) % count)
            return carry

        lax.fori_loop(1, count, step, 0)

    local(q_hbm, qg.at[0], in_sem.at[0])
    local(g_hbm, qg.at[1], in_sem.at[1])
    local(kv_hbm, kv, in_sem.at[2])

    barrier = pltpu.get_barrier_semaphore()

    def greet(where):
        pl.semaphore_signal(barrier, inc=1, device_id=where, device_id_type=MESH)

    others(A, a, lambda x: greet(on_a(x)))
    others(B, b, lambda x: greet(on_b(x)))
    others(H, j, lambda x: greet({"head": x}))

    tag[...] = jnp.zeros(tag.shape, jnp.int32)
    tag[0:1, 0 : tseg_v.shape[1]] = tseg_v[...]
    tag[1:2, 0 : mask_v.shape[1]] = mask_v[...]
    column = jnp.broadcast_to(pair_v[...], (n_ctx, n_ctx)).T
    here = lax.broadcasted_iota(jnp.int32, (n_ctx, n_ctx), 1)
    source = lax.broadcasted_iota(jnp.int32, (n_ctx, n_ctx), 0)
    inv_v[...] = jnp.max(jnp.where(column == here, source, 0), axis=0, keepdims=True)
    local(inv_v, inv_s, inv_sem)

    pl.semaphore_wait(barrier, A + B + H - 3)
    wait(qg.at[0], in_sem.at[0])
    wait(qg.at[1], in_sem.at[1])

    def start_s1(i):
        others(A, a, lambda x: send(qg.at[:, rows(x), cols(i)], s1.at[a, :, :, cols(i)], s1s.at[i], s1r.at[i], on_a(x)))
        local(qg.at[:, rows(a), cols(i)], s1.at[a, :, :, cols(i)], s1r.at[i])

    start_s1(0)
    others(A, a, lambda x: send(tag, ta.at[a], tas, tar, on_a(x)))
    local(tag, ta.at[a], tar)
    for i in range(1, len(GROUPS)):
        start_s1(i)

    for n in range(frames // BLOCK):
        fcol[n * BLOCK : (n + 1) * BLOCK, :] = jnp.broadcast_to(
            fseg_v[n : n + 1, :].astype(jnp.float32), (BLOCK, BLOCK)
        ).T

    def stage_s2(i):
        wait(s1.at[:, :, :, cols(i)], s1r.at[i])
        for kind in range(2):
            to = text_member(i, kind)
            src = s1.at[:, kind, :, cols(i)]
            dst = s2.at[:, b, :, cols(i)]

            @pl.when(to != b)
            def _():
                send(src, dst, s2s.at[i, kind], s2r.at[i], on_b(to))

            @pl.when(to == b)
            def _():
                local(src, dst, s2r.at[i])

        if i == 0:
            wait(ta, tar)
            others(B, b, lambda x: send(ta, tb.at[:, b], tbs, tbr, on_b(x)))
            local(ta, tb.at[:, b], tbr)
            wait(inv_v, inv_sem)

    def place(s):
        return (s // B) & (A - 1), s & (B - 1)

    def reorder(table, i, src, dst):
        def step(n, carry):
            for m in range(A):
                row, col = place(table(m * B + n))
                dst[n, m, :, cols(i)] = src[row, col, :, cols(i)]
            return carry

        lax.fori_loop(0, B, step, 0)

    def stage_s3(i):
        kind = (b == text_member(i, 1)).astype(jnp.int32)

        @pl.when((b == text_member(i, 0)) | (b == text_member(i, 1)))
        def _():
            wait(s2.at[:, :, :, cols(i)], s2r.at[i])
            reorder(lambda n: inv_s[0, n], i, s2, p3)
            others(B, b, lambda x: send(p3.at[x, :, :, cols(i)], s3.at[kind, :, :, cols(i)], s3s.at[i], s3r.at[i], on_b(x)))
            local(p3.at[b, :, :, cols(i)], s3.at[kind, :, :, cols(i)], s3r.at[i])

    def stage_s4(i):
        wait(s3.at[:, :, :, cols(i)], s3r.at[i])
        others(A, a, lambda x: send(s3.at[:, x, :, cols(i)], qr.at[:, rows(a), cols(i)], s4s.at[i], s4r.at[i], on_a(x)))
        local(s3.at[:, a, :, cols(i)], qr.at[:, rows(a), cols(i)], s4r.at[i])

    def attend(h):
        at = slice(h * DH, (h + 1) * DH)
        q = qr[0, :, at]
        g = qr[1, :, at]
        k = kv[0, :, at]
        v = kv[1, :, at]
        row, col = place(inv_s[0, c])
        tags = tb[row, col]
        ids = tags[0:1, 0 : q.shape[0]].astype(jnp.float32)
        scores = _dot(k, q, 1, 1) * scale
        parts = []
        for n in range(frames // BLOCK):
            open_ = jnp.broadcast_to(tags[1:2, n : n + 1], ids.shape) == 1
            wanted = jnp.where(open_, ids, -1.0)
            at_n = slice(n * BLOCK, (n + 1) * BLOCK)
            allowed = fcol[at_n, 0 : q.shape[0]] == wanted
            parts.append(jnp.where(allowed, scores[at_n, :], -1e30))
        masked = jnp.concatenate(parts, axis=0)
        logit = jnp.full((1, q.shape[0]), sink[h], jnp.float32)
        top = jnp.maximum(logit, jnp.max(masked, axis=0, keepdims=True))
        terms = jnp.exp(masked - top)
        total = jnp.exp(logit - top) + jnp.sum(terms, axis=0, keepdims=True)
        attention = terms * (1.0 / total)
        low = attention.astype(jnp.bfloat16)
        grad_attention = _dot(v, g, 1, 1)
        delta = jnp.sum(low.astype(jnp.float32) * grad_attention, axis=0, keepdims=True)
        grad_scores = (attention * (grad_attention - delta)).astype(jnp.bfloat16)
        dq[:, at] = (_dot(grad_scores, k, 0, 0) * scale).astype(jnp.bfloat16)
        dkv[0, :, at] = (_dot(grad_scores, q, 1, 0) * scale).astype(jnp.bfloat16)
        dkv[1, :, at] = _dot(low, g, 1, 0).astype(jnp.bfloat16)

    def stage_compute(i):
        first, count = GROUPS[i]
        if i == 0:
            wait(kv, in_sem.at[2])
            wait(tb, tbr)
        wait(qr.at[:, :, cols(i)], s4r.at[i])
        for h in range(first, first + count):
            attend(h)
        others(A, a, lambda x: send(dq.at[rows(x), cols(i)], r1.at[a, :, cols(i)], r1s.at[i], r1r.at[i], on_a(x)))
        local(dq.at[rows(a), cols(i)], r1.at[a, :, cols(i)], r1r.at[i])
        out_cols = pl.ds(pl.multiple_of((j * heads_here + first) * DH, DH), count * DH)

        def part(x):
            return dkv.at[:, pl.ds(pl.multiple_of(x * frame_part, frame_part), frame_part), cols(i)]

        others(H, j, lambda x: send(part(x), dkv_out.at[:, :, out_cols], ks.at[i], kr.at[i], {"head": x}))
        local(part(j), dkv_out.at[:, :, out_cols], kr.at[i])

    def stage_r2(i):
        wait(r1.at[:, :, cols(i)], r1r.at[i])
        to = grad_member(i)
        src = r1.at[:, :, cols(i)]
        dst = r2.at[:, b, :, cols(i)]

        @pl.when(to != b)
        def _():
            send(src, dst, r2s.at[i], r2r.at[i], on_b(to))

        @pl.when(to == b)
        def _():
            local(src, dst, r2r.at[i])

    def stage_r3(i):
        @pl.when(b == grad_member(i))
        def _():
            wait(r2.at[:, :, :, cols(i)], r2r.at[i])
            reorder(lambda n: pair_s[n], i, r2, rp)
            others(B, b, lambda x: send(rp.at[x, :, :, cols(i)], r3.at[:, :, cols(i)], r3s.at[i], r3r.at[i], on_b(x)))
            local(rp.at[b, :, :, cols(i)], r3.at[:, :, cols(i)], r3r.at[i])

    def stage_r4(i):
        wait(r3.at[:, :, cols(i)], r3r.at[i])
        others(A, a, lambda x: send(r3.at[x, :, cols(i)], dq_out.at[rows(a), cols(i)], r4s.at[i], r4r.at[i], on_a(x)))
        local(r3.at[a, :, cols(i)], dq_out.at[rows(a), cols(i)], r4r.at[i])

    stages = (stage_s2, stage_s3, stage_s4, stage_compute, stage_r2, stage_r3, stage_r4)
    for tick in range(len(GROUPS) + len(stages) - 1):
        for n in reversed(range(len(stages))):
            if 0 <= tick - n < len(GROUPS):
                stages[n](tick - n)

    wait(ta.at[0 : A - 1], tas)
    wait(tb.at[:, 0 : B - 1], tbs)
    for i in range(len(GROUPS)):
        wait(s1.at[0 : A - 1, :, :, cols(i)], s1s.at[i])
        for kind in range(2):

            @pl.when(text_member(i, kind) != b)
            def _():
                wait(s1.at[:, kind, :, cols(i)], s2s.at[i, kind])

        @pl.when((b == text_member(i, 0)) | (b == text_member(i, 1)))
        def _():
            wait(p3.at[0 : B - 1, :, :, cols(i)], s3s.at[i])

        wait(s3.at[:, 0 : A - 1, :, cols(i)], s4s.at[i])
        wait(dkv.at[:, 0 : (H - 1) * frame_part, cols(i)], ks.at[i])
        wait(dkv.at[:, :, cols(i)], kr.at[i])
        wait(r1.at[0 : A - 1, :, cols(i)], r1s.at[i])

        @pl.when(grad_member(i) != b)
        def _():
            wait(r1.at[:, :, cols(i)], r2s.at[i])

        @pl.when(b == grad_member(i))
        def _():
            wait(rp.at[0 : B - 1, :, :, cols(i)], r3s.at[i])

        wait(r3.at[0 : A - 1, :, cols(i)], r4s.at[i])
        wait(dq.at[:, cols(i)], r4r.at[i])


def shards(text_query, grad_out, frame_kv, sink_logit, pairing, block_mask, text_seg, frame_seg):
    n_ctx = lax.axis_size("ctx")
    H = lax.axis_size("head")
    text_rows, width = text_query.shape
    frames = frame_kv.shape[1]
    A = text_rows // TILE
    B = n_ctx // A
    n = len(GROUPS)
    bf = jnp.bfloat16
    dma = pltpu.SemaphoreType.DMA
    anywhere = pl.BlockSpec(memory_space=pl.ANY)
    vmem = pl.BlockSpec(memory_space=pltpu.VMEM)
    smem = pl.BlockSpec(memory_space=pltpu.SMEM)
    return pl.pallas_call(
        functools.partial(kernel, A, B, H),
        out_shape=(
            jax.ShapeDtypeStruct((text_rows, width), bf),
            jax.ShapeDtypeStruct((2, frames // H, width * H), bf),
        ),
        in_specs=[anywhere, anywhere, anywhere, smem, smem, vmem, vmem, vmem, vmem],
        out_specs=(anywhere, anywhere),
        scratch_shapes=[
            pltpu.VMEM((2, text_rows, width), bf),
            pltpu.VMEM((2, frames, width), bf),
            pltpu.VMEM((A, 2, TILE, width), bf),
            pltpu.VMEM((A, B, TILE, width), bf),
            pltpu.VMEM((B, A, TILE, width), bf),
            pltpu.VMEM((2, A, TILE, width), bf),
            pltpu.VMEM((2, text_rows, width), bf),
            pltpu.VMEM((2, frames, width), bf),
            pltpu.VMEM((text_rows, width), bf),
            pltpu.VMEM((A, TILE, width), bf),
            pltpu.VMEM((A, B, TILE, width), bf),
            pltpu.VMEM((B, A, TILE, width), bf),
            pltpu.VMEM((A, TILE, width), bf),
            pltpu.VMEM((2, 128), jnp.int32),
            pltpu.VMEM((A, 2, 128), jnp.int32),
            pltpu.VMEM((A, B, 2, 128), jnp.int32),
            pltpu.VMEM((frames, BLOCK), jnp.float32),
            pltpu.VMEM((1, n_ctx), jnp.int32),
            pltpu.SMEM((1, n_ctx), jnp.int32),
            dma((3,)),
            dma,
            dma((n,)), dma((n,)), dma((n, 2)), dma((n,)), dma((n,)), dma((n,)), dma((n,)), dma((n,)),
            dma((n,)), dma((n,)), dma((n,)), dma((n,)), dma((n,)), dma((n,)), dma((n,)), dma((n,)), dma((n,)), dma((n,)),
            dma, dma, dma, dma,
        ],
        compiler_params=pltpu.CompilerParams(
            collective_id=0, has_side_effects=True, vmem_limit_bytes=40 * 1024 * 1024
        ),
        name="paired_attention_grads",
    )(
        text_query,
        grad_out,
        frame_kv,
        sink_logit,
        pairing,
        pairing.reshape(1, n_ctx),
        block_mask,
        text_seg.reshape(1, text_rows),
        frame_seg.reshape(frames // BLOCK, BLOCK),
    )


def solution(mesh):
    in_specs = (
        P("ctx", "head"),
        P("ctx", "head"),
        P(None, "ctx", "head"),
        P("head"),
        P(),
        P("ctx", None),
        P("ctx"),
        P("ctx"),
    )
    out_specs = (P("ctx", "head"), P(None, ("ctx", "head"), None))
    return jax.shard_map(shards, mesh=mesh, in_specs=in_specs, out_specs=out_specs, check_vma=False)
```

time: 182 us -> 116 us (0.64)
  the two profiles are of different devices: /device:TPU:1 before, /device:TPU:8 now
where the time goes in v1:
time: 116 us
  Pallas kernels  107 us (92%)
  local copies, waits for them, and re-layouts  8.16 us (7%)
    pallas_call x1, Pallas kernels, shards(): pl.pallas_call(functools.partial(kernel, A, B, H), out_shape=(jax.ShapeDt...  107 us
    unnamed x18, local copies, waits for them, and re-layouts  8.16 us

profile of v1, /device:TPU:8, one launch (start us, length us, event | category | flops | bytes accessed | tf_op | source)
XLA Modules:
  0.0 115.8 jit_solution(1552478801438484255)
XLA Ops:
  0.6 0.0 copy-start
  0.6 1.3 %copy-done = bf16[2,512,640]{2,1,0:T(8,128)(2,1)S(1)} copy-done((bf16[2,512,640]{2,1,0:T(8,128)(2,1)S(1)}, bf16[2,512,640]{2,1,0:T(8,128)(2,1)}, u32[]{:S(2)}) %copy-start) | copy-done | bytes 1310744
  1.9 0.0 copy-start.1
  2.0 0.9 copy-done.1
  2.9 0.0 copy-start.2
  2.9 0.9 copy-done.2
  3.8 0.0 copy-start.3
  3.8 0.7 copy-done.3
  4.5 0.0 copy-start.4
  4.5 0.7 copy-done.4
  5.1 0.0 copy-start.5
  5.1 0.7 copy-done.5
  5.8 0.0 copy-start.6
  5.8 0.7 copy-done.6
  6.4 0.0 copy-start.7
  6.4 0.7 copy-done.7
  7.1 107.0 %paired_attention_grads.1 = (bf16[128,640]{1,0:T(8,128)(2,1)S(1)}, bf16[2,128,2560]{2,1,0:T(8,128)(2,1)S(1)}) custom-call(bf16[128,640]{1,0:T(8,128)(2,1)S(1)} %copy-done.1, bf16[128,640]{1,0:T(8,128)(2,1)S(1)} %copy-done.2, bf16[2,512,640]{2,1,0:T(8,128)(2,1)S(1)} %copy-done, f32[5]{0:T(128)S(1)} %copy-done.5, s32[128]{0:T(128)S(1)} %copy-done.4, ...), custom_call_target="tpu_custom_call" | custom-call | tf_op jit(solution)/shard_map/paired_attention_grads/pallas_call | solution.py:298
  114.1 0.7 copy.12
  114.8 1.1 copy.13
Async XLA Ops:
  0.6 1.3 %copy-start = (bf16[2,512,640]{2,1,0:T(8,128)(2,1)S(1)}, bf16[2,512,640]{2,1,0:T(8,128)(2,1)}, u32[]{:S(2)}) copy-start(bf16[2,512,640]{2,1,0:T(8,128)(2,1)} %kv_hbm.1) | copy-start | bytes 3932164
  1.9 0.9 copy-start.1
  2.9 0.9 copy-start.2
  3.8 0.7 copy-start.3
  4.5 0.7 copy-start.4
  5.1 0.7 copy-start.5
  5.8 0.7 copy-start.6
  6.4 0.7 copy-start.7

commit v2 on v1

v2 whole, which is shorter than its diff:
```python
import functools

import jax
import jax.numpy as jnp
from jax import lax
from jax.experimental import pallas as pl
from jax.experimental.pallas import tpu as pltpu
from jax.sharding import PartitionSpec as P

DH = 128
BLOCK = 128
TILE = 16
MESH = pl.DeviceIdType.MESH


def _dot(a, b, ca, cb):
    return lax.dot_general(a, b, (((ca,), (cb,)), ((), ())), preferred_element_type=jnp.float32)


def kernel(
    N, H,
    q_hbm, g_hbm, kv_hbm, sink_hbm, pair_hbm, mask_hbm, tseg_hbm, fseg_hbm,
    dq_out, dkv_out,
    qg, kv, arrived, ordered, qr, dkv, dq, tag, tags_in, tags_out, tag_here,
    fcol, sink, pair_s, pair_v, mask_v, tseg_v, fseg_v, inv_v, inv_s,
    in_sem, inv_sem,
    t1s, t1r, t2s, t2r, g1s, g1r, g2s, g2r, ks, kr, a1s, a1r, a2s, a2r,
):
    scale = DH ** (-0.5)
    c = lax.axis_index("ctx")
    j = lax.axis_index("head")
    text_rows = q_hbm.shape[0]
    heads_here = q_hbm.shape[1] // DH
    frames = kv_hbm.shape[1]
    frame_part = frames // H
    blocks = text_rows // TILE
    pieces = 2 * blocks
    text_roles = heads_here * pieces
    grad_roles = heads_here * blocks
    tag_role = text_roles + grad_roles
    core = j % 2

    def member(role):
        if N != 128:
            return jnp.where(core == 1, N - 1 - role, role)
        y, x, r = role & 7, (role >> 3) & 1, role >> 4
        r = jnp.where(core == 1, 7 - r, r)
        turned = ((r & 1) << 2) | (r & 2) | (r >> 2)
        return (y << 4) | (x << 3) | ((3 * y + 4 * x + turned) & 7)

    def role_of(device):
        if N != 128:
            return jnp.where(core == 1, N - 1 - device, device)
        y, x, z = device >> 4, (device >> 3) & 1, device & 7
        turned = (z + 32 - 3 * y - 4 * x) & 7
        r = ((turned & 1) << 2) | (turned & 2) | (turned >> 2)
        r = jnp.where(core == 1, 7 - r, r)
        return (r << 4) | (x << 3) | y

    role = role_of(c)
    is_text = role < text_roles
    is_grad = (role >= text_roles) & (role < tag_role)
    is_tag = role == tag_role

    def cols(h):
        return pl.ds(pl.multiple_of(h * DH, DH), DH)

    def rows(x):
        return pl.ds(pl.multiple_of(x * TILE, TILE), TILE)

    def send(src, dst, ssem, rsem, ctx):
        pltpu.make_async_remote_copy(
            src_ref=src, dst_ref=dst, send_sem=ssem, recv_sem=rsem, device_id={"ctx": ctx}, device_id_type=MESH
        ).start()

    def local(src, dst, sem):
        pltpu.make_async_copy(src, dst, sem).start()

    def wait(ref, sem):
        pltpu.make_async_copy(ref, ref, sem).wait()

    def loop(low, high, body):
        def step(k, carry):
            body(k)
            return carry

        lax.fori_loop(low, high, step, 0)

    def send_or_keep(src, dst, ssem, rsem, to):
        @pl.when(to != c)
        def _():
            send(src, dst, ssem, rsem, to)

        @pl.when(to == c)
        def _():
            local(src, dst, rsem)

    barrier = pltpu.get_barrier_semaphore()
    loop(1, N, lambda k: pl.semaphore_signal(barrier, inc=1, device_id={"ctx": (c + k) % N}, device_id_type=MESH))
    loop(1, H, lambda k: pl.semaphore_signal(barrier, inc=1, device_id={"head": (j + k) % H}, device_id_type=MESH))

    local(mask_hbm, mask_v, in_sem.at[3])
    local(tseg_hbm, tseg_v, in_sem.at[4])
    local(pair_hbm, pair_v, in_sem.at[5])
    local(q_hbm, qg.at[0], in_sem.at[0])
    local(g_hbm, qg.at[1], in_sem.at[1])
    local(pair_hbm, pair_s, in_sem.at[6])
    local(sink_hbm, sink, in_sem.at[7])
    local(fseg_hbm, fseg_v, in_sem.at[8])
    local(kv_hbm, kv, in_sem.at[2])

    tag[...] = jnp.zeros(tag.shape, jnp.int32)
    wait(mask_v, in_sem.at[3])
    wait(tseg_v, in_sem.at[4])
    wait(pair_v, in_sem.at[5])
    tag[0:1, 0:text_rows] = tseg_v[...]
    tag[1:2, 0 : mask_v.shape[1]] = mask_v[...]
    column = jnp.broadcast_to(pair_v[...], (N, N)).T
    here = lax.broadcasted_iota(jnp.int32, (N, N), 1)
    source = lax.broadcasted_iota(jnp.int32, (N, N), 0)
    inv_v[...] = jnp.max(jnp.where(column == here, source, 0), axis=0, keepdims=True)
    local(inv_v, inv_s, inv_sem)
    wait(fseg_v, in_sem.at[8])
    for n in range(frames // BLOCK):
        fcol[n * BLOCK : (n + 1) * BLOCK, :] = jnp.broadcast_to(
            fseg_v[n : n + 1, :].astype(jnp.float32), (BLOCK, BLOCK)
        ).T
    wait(inv_v, inv_sem)
    wait(pair_s, in_sem.at[6])
    wait(sink, in_sem.at[7])
    wait(qg.at[0], in_sem.at[0])
    wait(qg.at[1], in_sem.at[1])
    wait(kv, in_sem.at[2])
    pl.semaphore_wait(barrier, N + H - 2)

    send_or_keep(tag, tags_in.at[c], a1s, a1r, member(jnp.int32(tag_role)))
    for h in range(heads_here):

        def to_member(k):
            piece = (k + c) % pieces
            src = qg.at[piece // blocks, rows(piece % blocks), cols(h)]
            send_or_keep(src, arrived.at[c], t1s, t1r, member(h * pieces + piece))

        loop(0, pieces, to_member)

    def place(s):
        return s & (N - 1)

    def pass_on(table, src, dst, target, ssem, rsem):
        def step(n, carry):
            for m in range(8):
                to = (c + n * 8 + m) % N
                dst[to] = src[place(table[0, to])]
            for m in range(8):
                to = (c + n * 8 + m) % N
                send_or_keep(dst.at[to], target, ssem, rsem, to)
            return carry

        lax.fori_loop(0, N // 8, step, 0)

    @pl.when(is_tag)
    def _():
        wait(tags_in, a1r)
        pass_on(inv_s, tags_in, tags_out, tag_here, a2s, a2r)

    @pl.when(is_text)
    def _():
        head, piece = role // pieces, role % pieces
        wait(arrived, t1r)
        pass_on(inv_s, arrived, ordered, qr.at[piece // blocks, rows(piece % blocks), cols(head)], t2s, t2r.at[head])

    wait(tag_here, a2r)

    def attend(h):
        at = slice(h * DH, (h + 1) * DH)
        q = qr[0, :, at]
        g = qr[1, :, at]
        k = kv[0, :, at]
        v = kv[1, :, at]
        ids = tag_here[0:1, 0:text_rows].astype(jnp.float32)
        scores = _dot(k, q, 1, 1) * scale
        parts = []
        for n in range(frames // BLOCK):
            open_ = jnp.broadcast_to(tag_here[1:2, n : n + 1], ids.shape) == 1
            wanted = jnp.where(open_, ids, -1.0)
            at_n = slice(n * BLOCK, (n + 1) * BLOCK)
            allowed = fcol[at_n, 0:text_rows] == wanted
            parts.append(jnp.where(allowed, scores[at_n, :], -1e30))
        masked = jnp.concatenate(parts, axis=0)
        logit = jnp.full((1, text_rows), sink[0, h], jnp.float32)
        top = jnp.maximum(logit, jnp.max(masked, axis=0, keepdims=True))
        terms = jnp.exp(masked - top)
        total = jnp.exp(logit - top) + jnp.sum(terms, axis=0, keepdims=True)
        attention = terms * (1.0 / total)
        low = attention.astype(jnp.bfloat16)
        grad_attention = _dot(v, g, 1, 1)
        delta = jnp.sum(low.astype(jnp.float32) * grad_attention, axis=0, keepdims=True)
        grad_scores = (attention * (grad_attention - delta)).astype(jnp.bfloat16)
        dq[:, at] = (_dot(grad_scores, k, 0, 0) * scale).astype(jnp.bfloat16)

        def to_grad_member(n):
            block = (n + c) % blocks
            send_or_keep(
                dq.at[rows(block), at], arrived_grad.at[c], g1s, g1r, member(text_roles + h * blocks + block)
            )

        loop(0, blocks, to_grad_member)
        dkv[0, :, at] = (_dot(grad_scores, q, 1, 0) * scale).astype(jnp.bfloat16)
        dkv[1, :, at] = _dot(low, g, 1, 0).astype(jnp.bfloat16)
        out_cols = pl.ds(pl.multiple_of((j * heads_here + h) * DH, DH), DH)

        def part(x):
            return dkv.at[:, pl.ds(pl.multiple_of(x * frame_part, frame_part), frame_part), at]

        def to_peer(n):
            x = (j + n) % H
            pltpu.make_async_remote_copy(
                src_ref=part(x),
                dst_ref=dkv_out.at[:, :, out_cols],
                send_sem=ks,
                recv_sem=kr,
                device_id={"head": x},
                device_id_type=MESH,
            ).start()

        loop(1, H, to_peer)
        local(part(j), dkv_out.at[:, :, out_cols], kr)

    arrived_grad = arrived
    for h in range(heads_here):
        wait(qr.at[:, :, h * DH : (h + 1) * DH], t2r.at[h])
        attend(h)

    @pl.when(is_grad)
    def _():
        mine = role - text_roles
        wait(arrived, g1r)
        pass_on(pair_s, arrived, ordered, dq_out.at[rows(mine % blocks), cols(mine // blocks)], g2s, g2r)

    wait(dq, g2r)
    wait(dkv, kr)
    wait(dkv.at[:, 0 : (H - 1) * frame_part, :], ks)

    def sent(count, own, ssem):
        @pl.when(own)
        def _():
            wait(arrived.at[0 : count - 1], ssem)

        @pl.when(jnp.logical_not(own))
        def _():
            wait(arrived.at[0:count], ssem)

    sent(text_roles, is_text, t1s)
    sent(grad_roles, is_grad, g1s)

    @pl.when(jnp.logical_not(is_tag))
    def _():
        wait(tag, a1s)

    @pl.when(is_tag)
    def _():
        wait(tags_out.at[0 : N - 1], a2s)

    @pl.when(is_text)
    def _():
        wait(ordered.at[0 : N - 1], t2s)

    @pl.when(is_grad)
    def _():
        wait(ordered.at[0 : N - 1], g2s)


def shards(text_query, grad_out, frame_kv, sink_logit, pairing, block_mask, text_seg, frame_seg):
    N = lax.axis_size("ctx")
    H = lax.axis_size("head")
    text_rows, width = text_query.shape
    frames = frame_kv.shape[1]
    bf = jnp.bfloat16
    dma = pltpu.SemaphoreType.DMA
    hbm = pl.BlockSpec(memory_space=pltpu.HBM)
    return pl.pallas_call(
        functools.partial(kernel, N, H),
        out_shape=(
            jax.ShapeDtypeStruct((text_rows, width), bf),
            jax.ShapeDtypeStruct((2, frames // H, width * H), bf),
        ),
        in_specs=[hbm] * 8,
        out_specs=(hbm, hbm),
        scratch_shapes=[
            pltpu.VMEM((2, text_rows, width), bf),
            pltpu.VMEM((2, frames, width), bf),
            pltpu.VMEM((N, TILE, DH), bf),
            pltpu.VMEM((N, TILE, DH), bf),
            pltpu.VMEM((2, text_rows, width), bf),
            pltpu.VMEM((2, frames, width), bf),
            pltpu.VMEM((text_rows, width), bf),
            pltpu.VMEM((2, 128), jnp.int32),
            pltpu.VMEM((N, 2, 128), jnp.int32),
            pltpu.VMEM((N, 2, 128), jnp.int32),
            pltpu.VMEM((2, 128), jnp.int32),
            pltpu.VMEM((frames, BLOCK), jnp.float32),
            pltpu.SMEM((1, width // DH), jnp.float32),
            pltpu.SMEM((1, N), jnp.int32),
            pltpu.VMEM((1, N), jnp.int32),
            pltpu.VMEM((1, frames // BLOCK), jnp.int32),
            pltpu.VMEM((1, text_rows), jnp.int32),
            pltpu.VMEM((frames // BLOCK, BLOCK), jnp.int32),
            pltpu.VMEM((1, N), jnp.int32),
            pltpu.SMEM((1, N), jnp.int32),
            dma((9,)),
            dma,
            dma, dma, dma, dma((width // DH,)), dma, dma, dma, dma, dma, dma, dma, dma, dma, dma,
        ],
        compiler_params=pltpu.CompilerParams(
            collective_id=0, has_side_effects=True, vmem_limit_bytes=62 * 1024 * 1024
        ),
        name="paired_attention_grads",
    )(
        text_query,
        grad_out,
        frame_kv,
        sink_logit.reshape(1, width // DH),
        pairing.reshape(1, N),
        block_mask,
        text_seg.reshape(1, text_rows),
        frame_seg.reshape(frames // BLOCK, BLOCK),
    )


def solution(mesh):
    in_specs = (
        P("ctx", "head"),
        P("ctx", "head"),
        P(None, "ctx", "head"),
        P("head"),
        P(),
        P("ctx", None),
        P("ctx"),
        P("ctx"),
    )
    out_specs = (P("ctx", "head"), P(None, ("ctx", "head"), None))
    return jax.shard_map(shards, mesh=mesh, in_specs=in_specs, out_specs=out_specs, check_vma=False)
```

time: 116 us -> 73 us (0.63)
  the two profiles are of different devices: /device:TPU:8 before, /device:TPU:6 now
where the time goes in v2:
time: 73 us; the launch traced here: 72.8 us
  Pallas kernels  68.1 us (93%)
  local copies, waits for them, and re-layouts  4.05 us (6%)
    pallas_call x1, Pallas kernels, shards(): pl.pallas_call(functools.partial(kernel, N, H), out_shape=(jax.ShapeDtype...  68.1 us
    unnamed x2, local copies, waits for them, and re-layouts  4.05 us

profile of v2, /device:TPU:6, one launch (start us, length us, event | category | flops | bytes accessed | tf_op | source)
XLA Modules:
  0.0 72.8 jit_solution(10579453918631696803)
XLA Ops:
  0.6 68.1 %paired_attention_grads.1 = (bf16[128,640]{1,0:T(8,128)(2,1)}, bf16[2,128,2560]{2,1,0:T(8,128)(2,1)}) custom-call(bf16[128,640]{1,0:T(8,128)(2,1)} %q_hbm.1, bf16[128,640]{1,0:T(8,128)(2,1)} %g_hbm.1, bf16[2,512,640]{2,1,0:T(8,128)(2,1)} %kv_hbm.1, f32[1,5]{1,0:T(1,128)} %bitcast.5, s32[1,128]{1,0:T(1,128)} %bitcast.6, s32[1,4]{1,0:T(1,128)} %mask_hbm.1, ...), custom_call_target="tpu_custom_call" | custom-call | tf_op jit(solution)/shard_map/paired_attention_grads/pallas_call | solution.py:281
  68.7 1.6 %copy.12 = bf16[128,640]{1,0:T(8,128)(2,1)} copy(bf16[128,640]{1,0:T(8,128)(2,1)} %get-tuple-element.4) | data formatting | bytes 327680
  70.3 2.5 %copy.13 = bf16[2,128,2560]{2,1,0:T(8,128)(2,1)} copy(bf16[2,128,2560]{2,1,0:T(8,128)(2,1)} %get-tuple-element.5) | data formatting | bytes 2621440

commit v3 on v2

--- a/solution.py
+++ b/solution.py
@@ -9,7 +9,7 @@
 
 DH = 128
 BLOCK = 128
-TILE = 16
+TILE = 8
 MESH = pl.DeviceIdType.MESH
 
 
@@ -21,10 +21,10 @@
     N, H,
     q_hbm, g_hbm, kv_hbm, sink_hbm, pair_hbm, mask_hbm, tseg_hbm, fseg_hbm,
     dq_out, dkv_out,
-    qg, kv, arrived, ordered, qr, dkv, dq, tag, tags_in, tags_out, tag_here,
+    qg, kv, arrived, ordered, arrived_more, ordered_more, arrived_grad, ordered_grad, qr, dkv, dq, tag, tags_in, tags_out, tag_here,
     fcol, sink, pair_s, pair_v, mask_v, tseg_v, fseg_v, inv_v, inv_s,
     in_sem, inv_sem,
-    t1s, t1r, t2s, t2r, g1s, g1r, g2s, g2r, ks, kr, a1s, a1r, a2s, a2r,
+    t1s, t1r, t2s, t2r, m1r, m2s, g1s, g1r, g2s, g2r, ks, kr, a1s, a1r, a2s, a2r,
 ):
     scale = DH ** (-0.5)
     c = lax.axis_index("ctx")
@@ -37,8 +37,11 @@
     pieces = 2 * blocks
     text_roles = heads_here * pieces
     grad_roles = heads_here * blocks
-    tag_role = text_roles + grad_roles
-    core = j % 2
+    more = max(text_roles - N, 0)
+    first_grad = N - grad_roles
+    tag_role = N // 4
+    core = j % 2 if N == 128 else 0
+    partner = (j + H // 2) % H
 
     def member(role):
         if N != 128:
@@ -59,8 +62,9 @@
 
     role = role_of(c)
     is_text = role < text_roles
-    is_grad = (role >= text_roles) & (role < tag_role)
+    is_grad = role >= first_grad
     is_tag = role == tag_role
+    is_more = role < more
 
     def cols(h):
         return pl.ds(pl.multiple_of(h * DH, DH), DH)
@@ -70,7 +74,7 @@
 
     def send(src, dst, ssem, rsem, ctx):
         pltpu.make_async_remote_copy(
-            src_ref=src, dst_ref=dst, send_sem=ssem, recv_sem=rsem, device_id={"ctx": ctx}, device_id_type=MESH
+            src_ref=src, dst_ref=dst, send_sem=ssem, recv_sem=rsem, device_id=(ctx, partner), device_id_type=MESH
         ).start()
 
     def local(src, dst, sem):
@@ -86,17 +90,8 @@
 
         lax.fori_loop(low, high, step, 0)
 
-    def send_or_keep(src, dst, ssem, rsem, to):
-        @pl.when(to != c)
-        def _():
-            send(src, dst, ssem, rsem, to)
-
-        @pl.when(to == c)
-        def _():
-            local(src, dst, rsem)
-
     barrier = pltpu.get_barrier_semaphore()
-    loop(1, N, lambda k: pl.semaphore_signal(barrier, inc=1, device_id={"ctx": (c + k) % N}, device_id_type=MESH))
+    loop(0, N, lambda k: pl.semaphore_signal(barrier, inc=1, device_id=((c + 37 * k) % N, partner), device_id_type=MESH))
     loop(1, H, lambda k: pl.semaphore_signal(barrier, inc=1, device_id={"head": (j + k) % H}, device_id_type=MESH))
 
     local(mask_hbm, mask_v, in_sem.at[3])
@@ -131,15 +126,28 @@
     wait(qg.at[0], in_sem.at[0])
     wait(qg.at[1], in_sem.at[1])
     wait(kv, in_sem.at[2])
-    pl.semaphore_wait(barrier, N + H - 2)
-
-    send_or_keep(tag, tags_in.at[c], a1s, a1r, member(jnp.int32(tag_role)))
+    pl.semaphore_wait(barrier, N + H - 1)
+
+    send(tag, tags_in.at[c], a1s, a1r, member(jnp.int32(tag_role)))
     for h in range(heads_here):
 
         def to_member(k):
             piece = (k + c) % pieces
+            slot = h * pieces + piece
             src = qg.at[piece // blocks, rows(piece % blocks), cols(h)]
-            send_or_keep(src, arrived.at[c], t1s, t1r, member(h * pieces + piece))
+            if (h + 1) * pieces <= N:
+                send(src, arrived.at[c], t1s, t1r, member(slot))
+            elif h * pieces >= N:
+                send(src, arrived_more.at[c], t1s, m1r, member(slot - N))
+            else:
+
+                @pl.when(slot < N)
+                def _():
+                    send(src, arrived.at[c], t1s, t1r, member(slot))
+
+                @pl.when(slot >= N)
+                def _():
+                    send(src, arrived_more.at[c], t1s, m1r, member(slot - N))
 
         loop(0, pieces, to_member)
 
@@ -149,11 +157,11 @@
     def pass_on(table, src, dst, target, ssem, rsem):
         def step(n, carry):
             for m in range(8):
-                to = (c + n * 8 + m) % N
+                to = (c + 37 * (n * 8 + m)) % N
                 dst[to] = src[place(table[0, to])]
             for m in range(8):
-                to = (c + n * 8 + m) % N
-                send_or_keep(dst.at[to], target, ssem, rsem, to)
+                to = (c + 37 * (n * 8 + m)) % N
+                send(dst.at[to], target, ssem, rsem, to)
             return carry
 
         lax.fori_loop(0, N // 8, step, 0)
@@ -163,11 +171,21 @@
         wait(tags_in, a1r)
         pass_on(inv_s, tags_in, tags_out, tag_here, a2s, a2r)
 
+    def text_pass(slot, src, dst, rsem, ssem):
+        head, piece = slot // pieces, slot % pieces
+        wait(src, rsem)
+        target = qr.at[piece // blocks, rows(piece % blocks), cols(head)]
+        pass_on(inv_s, src, dst, target, ssem, t2r.at[head])
+
     @pl.when(is_text)
     def _():
-        head, piece = role // pieces, role % pieces
-        wait(arrived, t1r)
-        pass_on(inv_s, arrived, ordered, qr.at[piece // blocks, rows(piece % blocks), cols(head)], t2s, t2r.at[head])
+        text_pass(role, arrived, ordered, t1r, t2s)
+
+    if more:
+
+        @pl.when(is_more)
+        def _():
+            text_pass(role + N, arrived_more, ordered_more, m1r, m2s)
 
     wait(tag_here, a2r)
 
@@ -200,8 +218,8 @@
 
         def to_grad_member(n):
             block = (n + c) % blocks
-            send_or_keep(
-                dq.at[rows(block), at], arrived_grad.at[c], g1s, g1r, member(text_roles + h * blocks + block)
+            send(
+                dq.at[rows(block), at], arrived_grad.at[c], g1s, g1r, member(first_grad + h * blocks + block)
             )
 
         loop(0, blocks, to_grad_member)
@@ -226,48 +244,41 @@
         loop(1, H, to_peer)
         local(part(j), dkv_out.at[:, :, out_cols], kr)
 
-    arrived_grad = arrived
     for h in range(heads_here):
         wait(qr.at[:, :, h * DH : (h + 1) * DH], t2r.at[h])
         attend(h)
 
     @pl.when(is_grad)
     def _():
-        mine = role - text_roles
-        wait(arrived, g1r)
-        pass_on(pair_s, arrived, ordered, dq_out.at[rows(mine % blocks), cols(mine // blocks)], g2s, g2r)
+        mine = role - first_grad
+        wait(arrived_grad, g1r)
+        pass_on(pair_s, arrived_grad, ordered_grad, dq_out.at[rows(mine % blocks), cols(mine // blocks)], g2s, g2r)
 
     wait(dq, g2r)
     wait(dkv, kr)
     wait(dkv.at[:, 0 : (H - 1) * frame_part, :], ks)
 
-    def sent(count, own, ssem):
-        @pl.when(own)
+    wait(qg, t1s)
+    wait(dq, g1s)
+    wait(tag, a1s)
+
+    @pl.when(is_tag)
+    def _():
+        wait(tags_out, a2s)
+
+    @pl.when(is_text)
+    def _():
+        wait(ordered, t2s)
+
+    if more:
+
+        @pl.when(is_more)
         def _():
-            wait(arrived.at[0 : count - 1], ssem)
-
-        @pl.when(jnp.logical_not(own))
-        def _():
-            wait(arrived.at[0:count], ssem)
-
-    sent(text_roles, is_text, t1s)
-    sent(grad_roles, is_grad, g1s)
-
-    @pl.when(jnp.logical_not(is_tag))
-    def _():
-        wait(tag, a1s)
-
-    @pl.when(is_tag)
-    def _():
-        wait(tags_out.at[0 : N - 1], a2s)
-
-    @pl.when(is_text)
-    def _():
-        wait(ordered.at[0 : N - 1], t2s)
+            wait(ordered_more, m2s)
 
     @pl.when(is_grad)
     def _():
-        wait(ordered.at[0 : N - 1], g2s)
+        wait(ordered_grad, g2s)
 
 
 def shards(text_query, grad_out, frame_kv, sink_logit, pairing, block_mask, text_seg, frame_seg):
@@ -291,6 +302,10 @@
             pltpu.VMEM((2, frames, width), bf),
             pltpu.VMEM((N, TILE, DH), bf),
             pltpu.VMEM((N, TILE, DH), bf),
+            pltpu.VMEM((N, TILE, DH), bf),
+            pltpu.VMEM((N, TILE, DH), bf),
+            pltpu.VMEM((N, TILE, DH), bf),
+            pltpu.VMEM((N, TILE, DH), bf),
             pltpu.VMEM((2, text_rows, width), bf),
             pltpu.VMEM((2, frames, width), bf),
             pltpu.VMEM((text_rows, width), bf),
@@ -309,21 +324,26 @@
             pltpu.SMEM((1, N), jnp.int32),
             dma((9,)),
             dma,
-            dma, dma, dma, dma((width // DH,)), dma, dma, dma, dma, dma, dma, dma, dma, dma, dma,
+            dma, dma, dma, dma((width // DH,)), dma, dma, dma, dma, dma, dma, dma, dma, dma, dma, dma, dma,
         ],
         compiler_params=pltpu.CompilerParams(
-            collective_id=0, has_side_effects=True, vmem_limit_bytes=62 * 1024 * 1024
+            collective_id=0, has_side_effects=True, vmem_limit_bytes=40 * 1024 * 1024
         ),
         name="paired_attention_grads",
     )(
-        text_query,
-        grad_out,
-        frame_kv,
-        sink_logit.reshape(1, width // DH),
-        pairing.reshape(1, N),
-        block_mask,
-        text_seg.reshape(1, text_rows),
-        frame_seg.reshape(frames // BLOCK, BLOCK),
+        *(
+            pltpu.with_memory_space_constraint(x, pltpu.HBM)
+            for x in (
+                text_query,
+                grad_out,
+                frame_kv,
+                sink_logit.reshape(1, width // DH),
+                pairing.reshape(1, N),
+                block_mask,
+                text_seg.reshape(1, text_rows),
+                frame_seg.reshape(frames // BLOCK, BLOCK),
+            )
+        )
     )
 
 

time: 73 us -> 66.1 us (0.905)
  the two profiles are of different devices: /device:TPU:6 before, /device:TPU:16 now
where the time goes in v3:
time: 66.1 us; the launch traced here: 65.9 us
  Pallas kernels  63.6 us (96%)
  local copies, waits for them, and re-layouts  1.72 us (3%)
    pallas_call x1, Pallas kernels, shards(): pl.pallas_call(functools.partial(kernel, N, H), out_shape=(jax.ShapeDtype...  63.6 us
    unnamed x2, local copies, waits for them, and re-layouts  1.72 us

profile of v3, /device:TPU:16, one launch (start us, length us, event | category | flops | bytes accessed | tf_op | source)
XLA Modules:
  0.0 65.9 jit_solution(8069492533394394768)
XLA Ops:
  0.6 63.6 %paired_attention_grads.1 = (bf16[128,640]{1,0:T(8,128)(2,1)S(1)}, bf16[2,128,2560]{2,1,0:T(8,128)(2,1)S(1)}) custom-call(bf16[128,640]{1,0:T(8,128)(2,1)} %q_hbm.1, bf16[128,640]{1,0:T(8,128)(2,1)} %g_hbm.1, bf16[2,512,640]{2,1,0:T(8,128)(2,1)} %kv_hbm.1, f32[1,5]{1,0:T(1,128)} %bitcast.5, s32[1,128]{1,0:T(1,128)} %bitcast.6, s32[1,4]{1,0:T(1,128)} %mask_hbm.1, ...), custom_call_target="tpu_custom_call" | custom-call | tf_op jit(solution)/shard_map/paired_attention_grads/pallas_call | solution.py:292
  64.2 0.7 %copy.12 = bf16[128,640]{1,0:T(8,128)(2,1)} copy(bf16[128,640]{1,0:T(8,128)(2,1)S(1)} %get-tuple-element.4) | data formatting | bytes 327680
  64.9 1.1 %copy.13 = bf16[2,128,2560]{2,1,0:T(8,128)(2,1)} copy(bf16[2,128,2560]{2,1,0:T(8,128)(2,1)S(1)} %get-tuple-element.5) | data formatting | bytes 2621440

commit v4 on v3

--- a/solution.py
+++ b/solution.py
@@ -22,7 +22,7 @@
     q_hbm, g_hbm, kv_hbm, sink_hbm, pair_hbm, mask_hbm, tseg_hbm, fseg_hbm,
     dq_out, dkv_out,
     qg, kv, arrived, ordered, arrived_more, ordered_more, arrived_grad, ordered_grad, qr, dkv, dq, tag, tags_in, tags_out, tag_here,
-    fcol, sink, pair_s, pair_v, mask_v, tseg_v, fseg_v, inv_v, inv_s,
+    low_kept, scores_kept, fcol, sink, pair_s, pair_v, mask_v, tseg_v, fseg_v, inv_v, inv_s,
     in_sem, inv_sem,
     t1s, t1r, t2s, t2r, m1r, m2s, g1s, g1r, g2s, g2r, ks, kr, a1s, a1r, a2s, a2r,
 ):
@@ -66,6 +66,17 @@
     is_tag = role == tag_role
     is_more = role < more
 
+    outer = 8 if N == 128 else 1
+
+    def far(i):
+        return 4 + (1 - 2 * (i % 2)) * ((i + 1) // 2)
+
+    def target_of(i, m):
+        if N != 128:
+            return (c + m) % N
+        y, x, z = c >> 4, (c >> 3) & 1, c & 7
+        return (((y + far(m // 2)) & 7) << 4) | (((x + m % 2) & 1) << 3) | ((z + far(i)) & 7)
+
     def cols(h):
         return pl.ds(pl.multiple_of(h * DH, DH), DH)
 
@@ -91,7 +102,12 @@
         lax.fori_loop(low, high, step, 0)
 
     barrier = pltpu.get_barrier_semaphore()
-    loop(0, N, lambda k: pl.semaphore_signal(barrier, inc=1, device_id=((c + 37 * k) % N, partner), device_id_type=MESH))
+
+    def greet(i):
+        for m in range(N // outer):
+            pl.semaphore_signal(barrier, inc=1, device_id=(target_of(i, m), partner), device_id_type=MESH)
+
+    loop(0, outer, greet)
     loop(1, H, lambda k: pl.semaphore_signal(barrier, inc=1, device_id={"head": (j + k) % H}, device_id_type=MESH))
 
     local(mask_hbm, mask_v, in_sem.at[3])
@@ -133,6 +149,8 @@
 
         def to_member(k):
             piece = (k + c) % pieces
+            if N == 128:
+                piece = (((c >> 4) + far(k // (pieces // 8))) & 7) + 8 * (k % (pieces // 8))
             slot = h * pieces + piece
             src = qg.at[piece // blocks, rows(piece % blocks), cols(h)]
             if (h + 1) * pieces <= N:
@@ -155,16 +173,15 @@
         return s & (N - 1)
 
     def pass_on(table, src, dst, target, ssem, rsem):
-        def step(n, carry):
-            for m in range(8):
-                to = (c + 37 * (n * 8 + m)) % N
+        def step(i):
+            for m in range(N // outer):
+                to = target_of(i, m)
                 dst[to] = src[place(table[0, to])]
-            for m in range(8):
-                to = (c + 37 * (n * 8 + m)) % N
+            for m in range(N // outer):
+                to = target_of(i, m)
                 send(dst.at[to], target, ssem, rsem, to)
-            return carry
-
-        lax.fori_loop(0, N // 8, step, 0)
+
+        loop(0, outer, step)
 
     @pl.when(is_tag)
     def _():
@@ -218,13 +235,20 @@
 
         def to_grad_member(n):
             block = (n + c) % blocks
+            if N == 128:
+                block = (((c >> 4) + far(n // (blocks // 8))) & 7) + 8 * (n % (blocks // 8))
             send(
                 dq.at[rows(block), at], arrived_grad.at[c], g1s, g1r, member(first_grad + h * blocks + block)
             )
 
         loop(0, blocks, to_grad_member)
-        dkv[0, :, at] = (_dot(grad_scores, q, 1, 0) * scale).astype(jnp.bfloat16)
-        dkv[1, :, at] = _dot(low, g, 1, 0).astype(jnp.bfloat16)
+        low_kept[h] = low
+        scores_kept[h] = grad_scores
+
+    def share(h):
+        at = slice(h * DH, (h + 1) * DH)
+        dkv[0, :, at] = (_dot(scores_kept[h], qr[0, :, at], 1, 0) * scale).astype(jnp.bfloat16)
+        dkv[1, :, at] = _dot(low_kept[h], qr[1, :, at], 1, 0).astype(jnp.bfloat16)
         out_cols = pl.ds(pl.multiple_of((j * heads_here + h) * DH, DH), DH)
 
         def part(x):
@@ -247,6 +271,7 @@
     for h in range(heads_here):
         wait(qr.at[:, :, h * DH : (h + 1) * DH], t2r.at[h])
         attend(h)
+        share(h)
 
     @pl.when(is_grad)
     def _():
@@ -313,6 +338,8 @@
             pltpu.VMEM((N, 2, 128), jnp.int32),
             pltpu.VMEM((N, 2, 128), jnp.int32),
             pltpu.VMEM((2, 128), jnp.int32),
+            pltpu.VMEM((width // DH, frames, text_rows), bf),
+            pltpu.VMEM((width // DH, frames, text_rows), bf),
             pltpu.VMEM((frames, BLOCK), jnp.float32),
             pltpu.SMEM((1, width // DH), jnp.float32),
             pltpu.SMEM((1, N), jnp.int32),

time: 66.1 us -> 61.5 us (0.930)
  the two profiles are of different devices: /device:TPU:16 before, /device:TPU:8 now
where the time goes in v4:
time: 61.5 us; the launch traced here: 61.4 us
  Pallas kernels  59 us (96%)
  local copies, waits for them, and re-layouts  1.72 us (3%)
  between operations  0.64 us (1%)
    pallas_call x1, Pallas kernels, shards(): pl.pallas_call(functools.partial(kernel, N, H), out_shape=(jax.ShapeDtype...  59 us
    unnamed x2, local copies, waits for them, and re-layouts  1.72 us

profile of v4, /device:TPU:8, one launch (start us, length us, event | category | flops | bytes accessed | tf_op | source)
XLA Modules:
  0.0 61.4 jit_solution(10594967355195409814)
XLA Ops:
  0.6 59.0 %paired_attention_grads.1 = (bf16[128,640]{1,0:T(8,128)(2,1)S(1)}, bf16[2,128,2560]{2,1,0:T(8,128)(2,1)S(1)}) custom-call(bf16[128,640]{1,0:T(8,128)(2,1)} %q_hbm.1, bf16[128,640]{1,0:T(8,128)(2,1)} %g_hbm.1, bf16[2,512,640]{2,1,0:T(8,128)(2,1)} %kv_hbm.1, f32[1,5]{1,0:T(1,128)} %bitcast.5, s32[1,128]{1,0:T(1,128)} %bitcast.6, s32[1,4]{1,0:T(1,128)} %mask_hbm.1, ...), custom_call_target="tpu_custom_call" | custom-call | tf_op jit(solution)/shard_map/paired_attention_grads/pallas_call | solution.py:317
  59.7 0.7 %copy.12 = bf16[128,640]{1,0:T(8,128)(2,1)} copy(bf16[128,640]{1,0:T(8,128)(2,1)S(1)} %get-tuple-element.4) | data formatting | bytes 327680
  60.3 1.1 %copy.13 = bf16[2,128,2560]{2,1,0:T(8,128)(2,1)} copy(bf16[2,128,2560]{2,1,0:T(8,128)(2,1)S(1)} %get-tuple-element.5) | data formatting | bytes 2621440

commit v5 on v4

--- a/solution.py
+++ b/solution.py
@@ -39,7 +39,7 @@
     grad_roles = heads_here * blocks
     more = max(text_roles - N, 0)
     first_grad = N - grad_roles
-    tag_role = N // 4
+    tag_role = N - 1
     core = j % 2 if N == 128 else 0
     partner = (j + H // 2) % H
 

time: 61.5 us -> 62.4 us (1.015)
  Pallas kernels: 59 us -> 59.9 us
    pallas_call x1, Pallas kernels: 59 us -> 59.9 us  [shards(): pl.pallas_call(functools.partial(kernel, N, H), out_shape=(jax.ShapeDtype...]
where the time goes in v5:
time: 62.4 us; the launch traced here: 62.2 us
  Pallas kernels  59.9 us (96%)
  local copies, waits for them, and re-layouts  1.72 us (3%)
  between operations  0.64 us (1%)
    pallas_call x1, Pallas kernels, shards(): pl.pallas_call(functools.partial(kernel, N, H), out_shape=(jax.ShapeDtype...  59.9 us
    unnamed x2, local copies, waits for them, and re-layouts  1.72 us

profile of v5, /device:TPU:8, one launch (start us, length us, event | category | flops | bytes accessed | tf_op | source)
XLA Modules:
  0.0 62.2 jit_solution(9170844694803351077)
XLA Ops:
  0.6 59.9 %paired_attention_grads.1 = (bf16[128,640]{1,0:T(8,128)(2,1)S(1)}, bf16[2,128,2560]{2,1,0:T(8,128)(2,1)S(1)}) custom-call(bf16[128,640]{1,0:T(8,128)(2,1)} %q_hbm.1, bf16[128,640]{1,0:T(8,128)(2,1)} %g_hbm.1, bf16[2,512,640]{2,1,0:T(8,128)(2,1)} %kv_hbm.1, f32[1,5]{1,0:T(1,128)} %bitcast.5, s32[1,128]{1,0:T(1,128)} %bitcast.6, s32[1,4]{1,0:T(1,128)} %mask_hbm.1, ...), custom_call_target="tpu_custom_call" | custom-call | tf_op jit(solution)/shard_map/paired_attention_grads/pallas_call | solution.py:317
  60.5 0.7 %copy.12 = bf16[128,640]{1,0:T(8,128)(2,1)} copy(bf16[128,640]{1,0:T(8,128)(2,1)S(1)} %get-tuple-element.4) | data formatting | bytes 327680
  61.2 1.1 %copy.13 = bf16[2,128,2560]{2,1,0:T(8,128)(2,1)} copy(bf16[2,128,2560]{2,1,0:T(8,128)(2,1)S(1)} %get-tuple-element.5) | data formatting | bytes 2621440
